TPU v7x, 32 devices: a whole 2x2x4 slice. The times are simulated.
32 devices in a mesh: seq: 4 (over y, core), row: 4 (over z), col: 2 (over x).
Axes of the slice: x: 2, y: 2, z: 4, core: 2. Of those that a mesh axis runs over, the one named last changes fastest.
Arguments:
- tokens: bfloat16 [512, 6144], P('seq', 'row'), may hold values from -6 to 6
- weight: bfloat16 [6144, 24576], P('row', 'col'), may hold values from -0.078125 to 0.078125
- cotangent: bfloat16 [512, 24576], P(('seq', 'row'), 'col'), may hold values from -6 to 6
Outputs:
- activation: bfloat16 [512, 24576], P(('seq', 'row'), 'col')
- input_grad: bfloat16 [512, 6144], P('seq', 'row')
- weight_grad: bfloat16 [24576, 6144], P(('col', 'seq'), 'row')
All inputs are finite; a program needn't handle non-finite values.
Results may differ from a plain program's by a relative error of at most 0.02.
Values may be sent and summed in bfloat16 or wider, within the bound.
A program may use at most 128 MiB of HBM per device.

v0:
```python
import functools

import jax
import jax.numpy as jnp
from jax import lax
from jax.experimental import pallas as pl
from jax.experimental.pallas import tpu as pltpu
from jax.sharding import PartitionSpec as P

BF, F32 = jnp.bfloat16, jnp.float32
MESH = pl.DeviceIdType.MESH
ROOT = 0.7978845608028654
LAG = 1


def remote(src, dst, send, recv, device):
    return pltpu.make_async_remote_copy(
        src_ref=src, dst_ref=dst, send_sem=send, recv_sem=recv, device_id=device, device_id_type=MESH
    )


def kernel(S, R, NH, tok, w, cot, act, dall, tall, ig, wv, tokv, cotv, part, rbuf, dbuf, abuf, pre, igacc, igown,
           igs, igr, wsem, loc, tks, tkr, cts, ctr, rss, rsr, ags, agr, acs, acr, dsem, tsem, gss, gsr):
    s, r, c = lax.axis_index("seq"), lax.axis_index("row"), lax.axis_index("col")
    H = wv.shape[1]
    ck = H // NH
    m = cot.shape[0]
    T, F = tok.shape
    J = S * NH
    pair = 2 if S % 2 == 0 else 1

    def order(k):
        return jnp.where(k == 0, 0, 1 + k % max(S - 1, 1))

    def owner(k):
        i = order(k)
        return ((s // pair + i // pair) % (S // pair)) * pair + (s + i) % pair

    def reader(k):
        i = order(k)
        return ((s // pair + S // pair - i // pair) % (S // pair)) * pair + (s + i) % pair

    def at(seq=None, row=None, col=None):
        return (s if seq is None else seq, r if row is None else row, c if col is None else col)

    def cols(group, h=0, size=H):
        return pl.ds(pl.multiple_of(group * H + h * ck, 128), size)

    right, left = lax.rem(r + 1, R), lax.rem(r + R - 1, R)

    wcopy = [pltpu.make_async_copy(w.at[:, cols(s, h, ck)], wv.at[:, pl.ds(h * ck, ck)], wsem.at[h]) for h in range(NH)]
    own_tok = pltpu.make_async_copy(tok, tokv.at[0], loc.at[0])
    own_cot = pltpu.make_async_copy(cot.at[:, cols(s)], cotv.at[0], loc.at[1])
    own_tok.start()
    for cp in wcopy:
        cp.start()
    own_cot.start()

    barrier = pltpu.get_barrier_semaphore()

    def greet(device):
        pl.semaphore_signal(barrier, inc=1, device_id=device, device_id_type=MESH)

    for k in range(1, S):
        greet(at(seq=reader(k)))

    @pl.when(r > 0)
    def _():
        greet(at(row=left))

    @pl.when(r < R - 1)
    def _():
        greet(at(row=right))

    pl.semaphore_wait(barrier, (S - 1) + jnp.where(r > 0, 1, 0) + jnp.where(r < R - 1, 1, 0))

    def tok_copy(k):
        return remote(tok, tokv.at[k], tks.at[k], tkr.at[k], at(seq=reader(k)))

    def cot_copy(k):
        return remote(cot.at[:, cols(reader(k))], cotv.at[k], cts.at[k], ctr.at[k], at(seq=reader(k)))

    for k in range(1, S):
        tok_copy(k).start()
        cot_copy(k).start()

    def sum_right(j, o):
        return remote(part.at[j, o], rbuf.at[j, o], rss.at[j, o], rsr.at[j, o], at(row=right))

    def sum_left(j, o):
        slot = jnp.where(o == r - 1, R, o)
        return remote(part.at[j, o], rbuf.at[j, slot], rss.at[j, o], rsr.at[j, slot], at(row=left))

    def got_sum(j, slot):
        remote(part.at[j, 0], rbuf.at[j, slot], rss.at[j, 0], rsr.at[j, slot], at(row=right)).wait_recv()

    def d_right(j, o):
        return remote(dbuf.at[j, o], dbuf.at[j, o], ags.at[j, o], agr.at[j, o], at(row=right))

    def d_left(j, o):
        return remote(dbuf.at[j, o], dbuf.at[j, o], ags.at[j, jnp.where(o == r, R, o)], agr.at[j, o], at(row=left))

    def act_remote(j, k, h):
        return remote(abuf.at[j], act.at[:, cols(s, h, ck)], acs.at[j], acr.at[j], at(seq=owner(k)))

    def act_local(j, h):
        return pltpu.make_async_copy(abuf.at[j], act.at[:, cols(s, h, ck)], acr.at[j])

    def ig_copy(k):
        return remote(igs.at[k], igr.at[k], gss.at[k], gsr.at[k], at(seq=owner(k)))

    def tall_copy(k):
        return pltpu.make_async_copy(tokv.at[k], tall.at[k], tsem.at[k])

    def dall_copy(j, k, h):
        return pltpu.make_async_copy(dbuf.at[j], dall.at[k, :, :, pl.ds(pl.multiple_of(h * ck, 128), ck)], dsem.at[j])

    def each(n, fn):
        def body(i, carry):
            fn(i)
            return carry
        lax.fori_loop(0, n, body, 0)

    tile = 512 if ck % 512 == 0 else (384 if ck % 384 == 0 else 128)
    ftile = 512 if F % 512 == 0 else 128

    def project(j):
        k, h = j // NH, j % NH

        @pl.when(k == 0)
        def _():
            @pl.when(h == 0)
            def _():
                own_tok.wait()
            for i in range(NH):
                @pl.when(h == i)
                def _():
                    wcopy[i].wait()

        @pl.when((k > 0) & (h == 0))
        def _():
            tok_copy(k).wait_recv()

        @pl.when(h == 0)
        def _():
            tall_copy(k).start()

        def columns(i):
            here = pl.ds(pl.multiple_of(i * tile, 128), tile)
            there = pl.ds(pl.multiple_of(h * ck + i * tile, 128), tile)
            value = jnp.dot(tokv[k], wv[:, there], preferred_element_type=F32)
            part[j, :, :, here] = value.reshape(R, m, tile).astype(BF)

        each(ck // tile, columns)

        @pl.when(r == 0)
        def _():
            each(R - 1, lambda i: sum_right(j, R - 1 - i).start())

        @pl.when(r == R - 1)
        def _():
            each(R - 1, lambda i: sum_left(j, i).start())

    def far(o):
        return jnp.maximum(o, R - 1 - o)

    def add_right(j):
        def go(i):
            o = R - 1 - i

            @pl.when(o > r)
            def _():
                got_sum(j, o)
                part[j, o] = (part[j, o].astype(F32) + rbuf[j, o].astype(F32)).astype(BF)
                sum_right(j, o).start()
        each(R - 1, go)

    def add_left(j):
        def go(o):
            @pl.when(o < r)
            def _():
                got_sum(j, o)
                part[j, o] = (part[j, o].astype(F32) + rbuf[j, o].astype(F32)).astype(BF)
                sum_left(j, o).start()
        each(R - 1, go)

    def finish(j):
        k, h = j // NH, j % NH
        pre[...] = part[j, r].astype(F32)

        @pl.when(r > 0)
        def _():
            got_sum(j, r)
            pre[...] += rbuf[j, r].astype(F32)

        @pl.when(r < R - 1)
        def _():
            got_sum(j, R)
            pre[...] += rbuf[j, R].astype(F32)

        @pl.when((k == 0) & (h == 0))
        def _():
            own_cot.wait()

        @pl.when((k > 0) & (h == 0))
        def _():
            cot_copy(k).wait_recv()

        v = pre[...]
        sq = v * v
        t = jnp.tanh(ROOT * (v + 0.044715 * (sq * v)))
        half = 0.5 * (1.0 + t)
        slope = half + 0.5 * v * (1.0 - t * t) * (ROOT * (1.0 + (3 * 0.044715) * sq))
        ct = cotv[k, :, pl.ds(pl.multiple_of(h * ck, 128), ck)].astype(F32)
        dbuf[j, r] = (ct * slope).astype(BF)
        abuf[j] = (v * half).astype(BF)

        @pl.when(r < R - 1)
        def _():
            d_right(j, r).start()

        @pl.when(r > 0)
        def _():
            d_left(j, r).start()

        @pl.when(k == 0)
        def _():
            act_local(j, h).start()

        @pl.when(k > 0)
        def _():
            act_remote(j, k, h).start()

    def relay(t):
        def go(o):
            j = t - LAG * (far(o) + jnp.abs(r - o))

            @pl.when((o < r) & (j >= 0) & (j < J))
            def _():
                d_right(j, o).wait_recv()

                @pl.when(r < R - 1)
                def _():
                    d_right(j, o).start()

            @pl.when((o > r) & (j >= 0) & (j < J))
            def _():
                d_left(j, o).wait_recv()

                @pl.when(r > 0)
                def _():
                    d_left(j, o).start()

        each(R, go)

    def pull(j):
        k, h = j // NH, j % NH
        dall_copy(j, k, h).start()

        def features(i):
            here = pl.ds(pl.multiple_of(i * ftile, 128), ftile)
            grads = dbuf[j]
            if m % 16:
                grads = grads.astype(F32)
            grads = grads.reshape(R * m, ck).astype(BF)
            value = lax.dot_general(
                grads, wv[here, pl.ds(pl.multiple_of(h * ck, 128), ck)], (((1,), (1,)), ((), ())),
                preferred_element_type=F32,
            )

            @pl.when(h == 0)
            def _():
                igacc[:, here] = value

            @pl.when(h > 0)
            def _():
                igacc[:, here] += value

        each(F // ftile, features)

        @pl.when((h == NH - 1) & (k == 0))
        def _():
            igown[...] = igacc[...]

        @pl.when((h == NH - 1) & (k > 0))
        def _():
            igs[k] = igacc[...].astype(BF)
            ig_copy(k).start()

    def at_step(j, ok, fn):
        @pl.when(ok & (j >= 0) & (j < J))
        def _():
            fn(j)

    def step(t):
        at_step(t, True, project)
        at_step(t - LAG * (R - 1 + far(r)) - 1, True, pull)
        at_step(t - LAG * r, r > 0, add_right)
        at_step(t - LAG * (R - 1 - r), r < R - 1, add_left)
        at_step(t - LAG * far(r), True, finish)
        relay(t)

    each(J + LAG * 2 * (R - 1) + 1, step)

    for k in range(1, S):
        ig_copy(k).wait_recv()
        igown[...] += igr[k].astype(F32)
    ig[...] = igown[...].astype(BF)

    for k in range(1, S):
        tok_copy(k).wait_send()
        cot_copy(k).wait_send()
        ig_copy(k).wait_send()
    for k in range(S):
        tall_copy(k).wait()

    def drain(j):
        k, h = j // NH, j % NH
        dall_copy(j, k, h).wait()

        @pl.when(k == 0)
        def _():
            act_local(j, h).wait()

        @pl.when(k > 0)
        def _():
            act_remote(j, k, h).wait()

        def block(o):
            @pl.when(o > r)
            def _():
                sum_right(j, o).wait_send()

                @pl.when(r > 0)
                def _():
                    d_left(j, o).wait_send()

            @pl.when(o < r)
            def _():
                sum_left(j, o).wait_send()

                @pl.when(r < R - 1)
                def _():
                    d_right(j, o).wait_send()

        each(R, block)

        @pl.when(r < R - 1)
        def _():
            d_right(j, r).wait_send()

        @pl.when(r > 0)
        def _():
            d_left(j, r).wait_send()

    each(J, drain)


def solution(mesh):
    S, R, C = (mesh.shape[name] for name in ("seq", "row", "col"))

    def shards(tokens, weight, cotangent):
        T, F = tokens.shape
        H = weight.shape[1] // S
        m = cotangent.shape[0]
        NH = next(n for n in (3, 1) if n == 1 or (H % (n * 128) == 0 and H >= 512 * n))
        J, ck = S * NH, H // NH
        dma = pltpu.SemaphoreType.DMA
        anywhere = pl.BlockSpec(memory_space=pl.ANY)
        act, dall, tall, ig = pl.pallas_call(
            functools.partial(kernel, S, R, NH),
            out_shape=(
                jax.ShapeDtypeStruct((m, S * H), BF),
                jax.ShapeDtypeStruct((S, R, m, H), BF),
                jax.ShapeDtypeStruct((S, T, F), BF),
                jax.ShapeDtypeStruct((T, F), BF),
            ),
            in_specs=[anywhere] * 3,
            out_specs=(anywhere, anywhere, anywhere, pl.BlockSpec(memory_space=pltpu.VMEM)),
            scratch_shapes=[
                pltpu.VMEM((F, H), BF),
                pltpu.VMEM((S, T, F), BF),
                pltpu.VMEM((S, m, H), BF),
                pltpu.VMEM((J, R, m, ck), BF),
                pltpu.VMEM((J, R + 1, m, ck), BF),
                pltpu.VMEM((J, R, m, ck), BF),
                pltpu.VMEM((J, m, ck), BF),
                pltpu.VMEM((m, ck), F32),
                pltpu.VMEM((T, F), F32),
                pltpu.VMEM((T, F), F32),
                pltpu.VMEM((S, T, F), BF),
                pltpu.VMEM((S, T, F), BF),
                dma((NH,)),
                dma((2,)),
                dma((S,)), dma((S,)), dma((S,)), dma((S,)),
                dma((J, R)), dma((J, R + 1)), dma((J, R + 1)), dma((J, R)),
                dma((J,)), dma((J,)), dma((J,)), dma((S,)),
                dma((S,)), dma((S,)),
            ],
            compiler_params=pltpu.CompilerParams(
                collective_id=0, has_side_effects=True, vmem_limit_bytes=60 * 1024 * 1024
            ),
        )(tokens, weight, cotangent)
        if C == 2:
            other = lax.ppermute(ig, "col", [(0, 1), (1, 0)])
            total = (ig.astype(F32) + other.astype(F32)).astype(BF)
        else:
            total = lax.psum(ig, "col")
        grad = lax.dot_general(
            dall.reshape(S * T, H), tall.reshape(S * T, F), (((0,), (0,)), ((), ())), preferred_element_type=F32
        ).astype(BF)
        return act, total, grad

    in_specs = (P("seq", "row"), P("row", "col"), P(("seq", "row"), "col"))
    out_specs = (P(("seq", "row"), "col"), P("seq", "row"), P(("col", "seq"), "row"))
    return jax.shard_map(shards, mesh=mesh, in_specs=in_specs, out_specs=out_specs, check_vma=False)
```

profile of v0, /device:TPU:0, one launch (start us, length us, event | category | flops | bytes accessed | tf_op | source)
XLA Modules:
  0.0 109.5 jit_solution(5988565614409506602)
XLA Ops:
  0.6 95.2 %shard_map.58 = (bf16[32,12288]{1,0:T(8,128)(2,1)}, bf16[4,4,32,3072]{3,2,1,0:T(8,128)(2,1)}, bf16[4,128,1536]{2,1,0:T(8,128)(2,1)}, bf16[128,1536]{1,0:T(8,128)(2,1)}) custom-call(bf16[128,1536]{1,0:T(8,128)(2,1)} %tok.1, bf16[1536,12288]{1,0:T(8,128)(2,1)} %w.1, bf16[32,12288]{1,0:T(8,128)(2,1)} %cot.1), custom_call_target="tpu_custom_call" | custom-call | tf_op jit(solution)/shard_map/pallas_call | solution.py:370
  95.8 1.5 %collective-permute-start = (bf16[128,1536]{1,0:T(8,128)(2,1)}, bf16[128,1536]{1,0:T(8,128)(2,1)S(1)}, u32[]{:S(2)}, u32[]{:S(2)}) collective-permute-start(bf16[128,1536]{1,0:T(8,128)(2,1)} %get-tuple-element.8), channel_id=1, source_target_pairs={{0,1},{1,0},{2,3},{3,2},{4,5},{5,4},{6,7},{7,6},{8,9},{9,8},{10,11... | collective-permute-start | bytes 1179656 | tf_op jit(solution)/shard_map/ppermute | solution.py:405
  97.4 0.0 copy-start.1
  97.4 0.0 copy-start
  97.4 9.5 %convolution_convert_fusion = bf16[3072,1536]{1,0:T(8,128)(2,1)} fusion(bf16[512,3072]{1,0:T(8,128)(2,1)} %bitcast.4, bf16[512,1536]{1,0:T(8,128)(2,1)} %bitcast.5), kind=kOutput, calls=%fused_computation | convolution fusion | flops 4836556800 | bytes 14155776 | tf_op jit(solution)/shard_map/dot_general | solution.py:409
  106.9 0.9 collective-permute-done
  107.7 0.0 copy-done.1
  107.7 0.8 add_convert_fusion
  108.6 0.0 copy-done
  108.6 0.9 copy.7
Async XLA Ops:
  95.8 11.9 %collective-permute-start = (bf16[128,1536]{1,0:T(8,128)(2,1)}, bf16[128,1536]{1,0:T(8,128)(2,1)S(1)}, u32[]{:S(2)}, u32[]{:S(2)}) collective-permute-start(bf16[128,1536]{1,0:T(8,128)(2,1)} %get-tuple-element.8), channel_id=1, source_target_pairs={{0,1},{1,0},{2,3},{3,2},{4,5},{5,4},{6,7},{7,6},{8,9},{9,8},{10,11... | collective-permute-start | bytes 1179656 | tf_op jit(solution)/shard_map/ppermute | solution.py:405
  97.4 10.4 %copy-start.1 = (bf16[128,1536]{1,0:T(8,128)(2,1)S(1)}, bf16[128,1536]{1,0:T(8,128)(2,1)}, u32[]{:S(2)}) copy-start(bf16[128,1536]{1,0:T(8,128)(2,1)} %get-tuple-element.8) | copy-start | bytes 1179652
  97.4 11.2 %copy-start = (bf16[32,12288]{1,0:T(8,128)(2,1)S(1)}, bf16[32,12288]{1,0:T(8,128)(2,1)}, u32[]{:S(2)}) copy-start(bf16[32,12288]{1,0:T(8,128)(2,1)} %get-tuple-element.14) | copy-start | bytes 2359300
where the time goes:
time: 110 us; the launch traced here: 109 us
  Pallas kernels  95.2 us (87%)
  matrix products  9.47 us (9%)
  starting transfers between devices  1.55 us (1%)
    pallas_call x1, Pallas kernels, shards(): pl.pallas_call(functools.partial(kernel, S, R, NH), out_shape=(jax.ShapeD...  95.2 us
    dot_general x1, matrix products, shards(): lax.dot_general(dall.reshape(S * T, H), tall.reshape(S * T, F), (((0,), (...  9.47 us
  transfers between devices with their start and end apart: 1, of which 1 were waited for; matrix products, arithmetic and copies ran while one was open for 9% of the time, Pallas kernels for 0%

commit v1 on v0

--- a/solution.py
+++ b/solution.py
@@ -11,6 +11,7 @@
 MESH = pl.DeviceIdType.MESH
 ROOT = 0.7978845608028654
 LAG = 1
+PIECES = {1: 3, 2: 2}
 
 
 def remote(src, dst, send, recv, device):
@@ -19,14 +20,22 @@
     )
 
 
-def kernel(S, R, NH, tok, w, cot, act, dall, tall, ig, wv, tokv, cotv, part, rbuf, dbuf, abuf, pre, igacc, igown,
-           igs, igr, wsem, loc, tks, tkr, cts, ctr, rss, rsr, ags, agr, acs, acr, dsem, tsem, gss, gsr):
+def kernel(S, R, NH, Q, *refs):
+    outs = 6 if Q > 1 else 4
+    tok, w, cot = refs[:3]
+    act, dall, tall, ig = refs[3:7]
+    (wv, tokv, cotv, part, rbuf, dbuf, abuf, pre, igacc, igown, igs, igr, wsem, loc, tks, tkr, cts, ctr, rss, rsr, ags,
+     agr, acs, acr, dsem, tsem, gss, gsr) = refs[3 + outs:31 + outs]
+    if Q > 1:
+        early, wearly = refs[7:9]
+        wst, xs, xr, xsem, wout = refs[31 + outs:]
     s, r, c = lax.axis_index("seq"), lax.axis_index("row"), lax.axis_index("col")
     H = wv.shape[1]
     ck = H // NH
-    m = cot.shape[0]
+    m = cot.shape[0] // Q
     T, F = tok.shape
-    J = S * NH
+    U = R * m
+    J = Q * S * NH
     pair = 2 if S % 2 == 0 else 1
 
     def order(k):
@@ -45,6 +54,23 @@
 
     def cols(group, h=0, size=H):
         return pl.ds(pl.multiple_of(group * H + h * ck, 128), size)
+
+    def unit(j):
+        u = j // NH
+        q, k = u // S, u % S
+        if Q > 1:
+            k = jnp.where(q == Q - 1, (k + 1) % S, k)
+        return q, k, j % NH
+
+    def rows(q):
+        return pl.ds(pl.multiple_of(q * m, m), m)
+
+    def tokens_of(k, q):
+        if Q == 1:
+            return tokv[k]
+        return jnp.concatenate(
+            [tokv[k, pl.ds(pl.multiple_of((o * Q + q) * m, m), m), :] for o in range(R)], axis=0
+        )
 
     right, left = lax.rem(r + 1, R), lax.rem(r + R - 1, R)
 
@@ -72,7 +98,10 @@
     def _():
         greet(at(row=right))
 
-    pl.semaphore_wait(barrier, (S - 1) + jnp.where(r > 0, 1, 0) + jnp.where(r < R - 1, 1, 0))
+    if Q > 1:
+        greet(at(col=1 - c))
+
+    pl.semaphore_wait(barrier, (S - 1) + (1 if Q > 1 else 0) + jnp.where(r > 0, 1, 0) + jnp.where(r < R - 1, 1, 0))
 
     def tok_copy(k):
         return remote(tok, tokv.at[k], tks.at[k], tkr.at[k], at(seq=reader(k)))
@@ -100,17 +129,29 @@
     def d_left(j, o):
         return remote(dbuf.at[j, o], dbuf.at[j, o], ags.at[j, jnp.where(o == r, R, o)], agr.at[j, o], at(row=left))
 
-    def act_remote(j, k, h):
-        return remote(abuf.at[j], act.at[:, cols(s, h, ck)], acs.at[j], acr.at[j], at(seq=owner(k)))
-
-    def act_local(j, h):
-        return pltpu.make_async_copy(abuf.at[j], act.at[:, cols(s, h, ck)], acr.at[j])
-
-    def ig_copy(k):
-        return remote(igs.at[k], igr.at[k], gss.at[k], gsr.at[k], at(seq=owner(k)))
-
-    def tall_copy(k):
-        return pltpu.make_async_copy(tokv.at[k], tall.at[k], tsem.at[k])
+    def act_remote(j, q, k, h):
+        return remote(abuf.at[j], act.at[rows(q), cols(s, h, ck)], acs.at[j], acr.at[j], at(seq=owner(k)))
+
+    def act_local(j, q, h):
+        return pltpu.make_async_copy(abuf.at[j], act.at[rows(q), cols(s, h, ck)], acr.at[j])
+
+    def ig_copy(q, k):
+        return remote(igs.at[q, k], igr.at[q, k], gss.at[q, k], gsr.at[q, k], at(seq=owner(k)))
+
+    def x_copy():
+        return remote(xs, xr, xsem.at[0], xsem.at[1], at(col=1 - c))
+
+    def early_copy(h):
+        return pltpu.make_async_copy(
+            wst.at[pl.ds(pl.multiple_of(h * ck, 128), ck)], wearly.at[pl.ds(pl.multiple_of(h * ck, 128), ck)], wout.at[h]
+        )
+
+    def tall_copy(k, o):
+        if Q == 1:
+            return pltpu.make_async_copy(tokv.at[k], tall.at[k], tsem.at[k, o])
+        return pltpu.make_async_copy(
+            tokv.at[k, pl.ds((o * Q + Q - 1) * m, m), :], tall.at[k, pl.ds(o * m, m), :], tsem.at[k, o]
+        )
 
     def dall_copy(j, k, h):
         return pltpu.make_async_copy(dbuf.at[j], dall.at[k, :, :, pl.ds(pl.multiple_of(h * ck, 128), ck)], dsem.at[j])
@@ -125,9 +166,9 @@
     ftile = 512 if F % 512 == 0 else 128
 
     def project(j):
-        k, h = j // NH, j % NH
-
-        @pl.when(k == 0)
+        q, k, h = unit(j)
+
+        @pl.when((q == 0) & (k == 0))
         def _():
             @pl.when(h == 0)
             def _():
@@ -137,18 +178,19 @@
                 def _():
                     wcopy[i].wait()
 
-        @pl.when((k > 0) & (h == 0))
+        @pl.when((q == 0) & (k > 0) & (h == 0))
         def _():
             tok_copy(k).wait_recv()
 
-        @pl.when(h == 0)
-        def _():
-            tall_copy(k).start()
+        @pl.when((q == 0) & (h == 0))
+        def _():
+            for o in range(R if Q > 1 else 1):
+                tall_copy(k, o).start()
 
         def columns(i):
             here = pl.ds(pl.multiple_of(i * tile, 128), tile)
             there = pl.ds(pl.multiple_of(h * ck + i * tile, 128), tile)
-            value = jnp.dot(tokv[k], wv[:, there], preferred_element_type=F32)
+            value = jnp.dot(tokens_of(k, q), wv[:, there], preferred_element_type=F32)
             part[j, :, :, here] = value.reshape(R, m, tile).astype(BF)
 
         each(ck // tile, columns)
@@ -185,7 +227,7 @@
         each(R - 1, go)
 
     def finish(j):
-        k, h = j // NH, j % NH
+        q, k, h = unit(j)
         pre[...] = part[j, r].astype(F32)
 
         @pl.when(r > 0)
@@ -198,11 +240,11 @@
             got_sum(j, R)
             pre[...] += rbuf[j, R].astype(F32)
 
-        @pl.when((k == 0) & (h == 0))
+        @pl.when((q == 0) & (k == 0) & (h == 0))
         def _():
             own_cot.wait()
 
-        @pl.when((k > 0) & (h == 0))
+        @pl.when((q == 0) & (k > 0) & (h == 0))
         def _():
             cot_copy(k).wait_recv()
 
@@ -211,7 +253,7 @@
         t = jnp.tanh(ROOT * (v + 0.044715 * (sq * v)))
         half = 0.5 * (1.0 + t)
         slope = half + 0.5 * v * (1.0 - t * t) * (ROOT * (1.0 + (3 * 0.044715) * sq))
-        ct = cotv[k, :, pl.ds(pl.multiple_of(h * ck, 128), ck)].astype(F32)
+        ct = cotv[k, rows(q), pl.ds(pl.multiple_of(h * ck, 128), ck)].astype(F32)
         dbuf[j, r] = (ct * slope).astype(BF)
         abuf[j] = (v * half).astype(BF)
 
@@ -225,11 +267,11 @@
 
         @pl.when(k == 0)
         def _():
-            act_local(j, h).start()
+            act_local(j, q, h).start()
 
         @pl.when(k > 0)
         def _():
-            act_remote(j, k, h).start()
+            act_remote(j, q, k, h).start()
 
     def relay(t):
         def go(o):
@@ -254,15 +296,18 @@
         each(R, go)
 
     def pull(j):
-        k, h = j // NH, j % NH
-        dall_copy(j, k, h).start()
+        q, k, h = unit(j)
+
+        @pl.when(q == Q - 1)
+        def _():
+            dall_copy(j, k, h).start()
 
         def features(i):
             here = pl.ds(pl.multiple_of(i * ftile, 128), ftile)
             grads = dbuf[j]
             if m % 16:
                 grads = grads.astype(F32)
-            grads = grads.reshape(R * m, ck).astype(BF)
+            grads = grads.reshape(U, ck).astype(BF)
             value = lax.dot_general(
                 grads, wv[here, pl.ds(pl.multiple_of(h * ck, 128), ck)], (((1,), (1,)), ((), ())),
                 preferred_element_type=F32,
@@ -280,12 +325,37 @@
 
         @pl.when((h == NH - 1) & (k == 0))
         def _():
-            igown[...] = igacc[...]
+            igown[q] = igacc[...]
 
         @pl.when((h == NH - 1) & (k > 0))
         def _():
-            igs[k] = igacc[...].astype(BF)
-            ig_copy(k).start()
+            igs[q, k] = igacc[...].astype(BF)
+            ig_copy(q, k).start()
+
+        if Q > 1:
+            @pl.when((q == 0) & (k == S - 1))
+            def _():
+                partial_grad(h)
+
+            @pl.when((q == Q - 1) & (k == S - 1) & (h == 0))
+            def _():
+                for i in range(1, S):
+                    ig_copy(0, i).wait_recv()
+                    igown[0] += igr[0, i].astype(F32)
+                xs[...] = igown[0].astype(BF)
+                x_copy().start()
+
+    def partial_grad(h):
+        def hidden(i):
+            here = pl.ds(pl.multiple_of(i * tile, 128), tile)
+            there = pl.ds(pl.multiple_of(h * ck + i * tile, 128), tile)
+            grads = jnp.concatenate([dbuf[k * NH + h, :, :, here].reshape(U, tile) for k in range(S)], axis=0)
+            toks = jnp.concatenate([tokens_of(k, 0) for k in range(S)], axis=0)
+            value = lax.dot_general(grads, toks, (((0,), (0,)), ((), ())), preferred_element_type=F32)
+            wst[there, :] = value.astype(BF)
+
+        each(ck // tile, hidden)
+        early_copy(h).start()
 
     def at_step(j, ok, fn):
         @pl.when(ok & (j >= 0) & (j < J))
@@ -303,28 +373,39 @@
     each(J + LAG * 2 * (R - 1) + 1, step)
 
     for k in range(1, S):
-        ig_copy(k).wait_recv()
-        igown[...] += igr[k].astype(F32)
-    ig[...] = igown[...].astype(BF)
+        ig_copy(Q - 1, k).wait_recv()
+        igown[Q - 1] += igr[Q - 1, k].astype(F32)
+    ig[...] = igown[Q - 1].astype(BF)
+    if Q > 1:
+        x_copy().wait_recv()
+        early[...] = (xs[...].astype(F32) + xr[...].astype(F32)).astype(BF)
+        x_copy().wait_send()
+        for h in range(NH):
+            early_copy(h).wait()
 
     for k in range(1, S):
         tok_copy(k).wait_send()
         cot_copy(k).wait_send()
-        ig_copy(k).wait_send()
+        for q in range(Q):
+            ig_copy(q, k).wait_send()
     for k in range(S):
-        tall_copy(k).wait()
+        for o in range(R if Q > 1 else 1):
+            tall_copy(k, o).wait()
 
     def drain(j):
-        k, h = j // NH, j % NH
-        dall_copy(j, k, h).wait()
+        q, k, h = unit(j)
+
+        @pl.when(q == Q - 1)
+        def _():
+            dall_copy(j, k, h).wait()
 
         @pl.when(k == 0)
         def _():
-            act_local(j, h).wait()
+            act_local(j, q, h).wait()
 
         @pl.when(k > 0)
         def _():
-            act_remote(j, k, h).wait()
+            act_remote(j, q, k, h).wait()
 
         def block(o):
             @pl.when(o > r)
@@ -362,41 +443,53 @@
     def shards(tokens, weight, cotangent):
         T, F = tokens.shape
         H = weight.shape[1] // S
-        m = cotangent.shape[0]
-        NH = next(n for n in (3, 1) if n == 1 or (H % (n * 128) == 0 and H >= 512 * n))
-        J, ck = S * NH, H // NH
+        Q = 2 if C == 2 and S > 2 and cotangent.shape[0] % 32 == 0 else 1
+        m = cotangent.shape[0] // Q
+        U = R * m
+        NH = next(n for n in (PIECES[Q], 1) if n == 1 or (H % (n * 128) == 0 and H >= 512 * n))
+        J, ck = Q * S * NH, H // NH
         dma = pltpu.SemaphoreType.DMA
         anywhere = pl.BlockSpec(memory_space=pl.ANY)
-        act, dall, tall, ig = pl.pallas_call(
-            functools.partial(kernel, S, R, NH),
-            out_shape=(
-                jax.ShapeDtypeStruct((m, S * H), BF),
-                jax.ShapeDtypeStruct((S, R, m, H), BF),
-                jax.ShapeDtypeStruct((S, T, F), BF),
-                jax.ShapeDtypeStruct((T, F), BF),
-            ),
+        inside = pl.BlockSpec(memory_space=pltpu.VMEM)
+        out_shape = [
+            jax.ShapeDtypeStruct((Q * m, S * H), BF),
+            jax.ShapeDtypeStruct((S, R, m, H), BF),
+            jax.ShapeDtypeStruct((S, U, F), BF),
+            jax.ShapeDtypeStruct((U, F), BF),
+        ]
+        out_specs = [anywhere, anywhere, anywhere, inside]
+        scratch = [
+            pltpu.VMEM((F, H), BF),
+            pltpu.VMEM((S, T, F), BF),
+            pltpu.VMEM((S, Q * m, H), BF),
+            pltpu.VMEM((J, R, m, ck), BF),
+            pltpu.VMEM((J, R + 1, m, ck), BF),
+            pltpu.VMEM((J, R, m, ck), BF),
+            pltpu.VMEM((J, m, ck), BF),
+            pltpu.VMEM((m, ck), F32),
+            pltpu.VMEM((U, F), F32),
+            pltpu.VMEM((Q, U, F), F32),
+            pltpu.VMEM((Q, S, U, F), BF),
+            pltpu.VMEM((Q, S, U, F), BF),
+            dma((NH,)),
+            dma((2,)),
+            dma((S,)), dma((S,)), dma((S,)), dma((S,)),
+            dma((J, R)), dma((J, R + 1)), dma((J, R + 1)), dma((J, R)),
+            dma((J,)), dma((J,)), dma((J,)), dma((S, R)),
+            dma((Q, S)), dma((Q, S)),
+        ]
+        if Q > 1:
+            out_shape += [jax.ShapeDtypeStruct((U, F), BF), jax.ShapeDtypeStruct((H, F), BF)]
+            out_specs += [inside, anywhere]
+            scratch += [
+                pltpu.VMEM((H, F), BF), pltpu.VMEM((U, F), BF), pltpu.VMEM((U, F), BF), dma((2,)), dma((NH,)),
+            ]
+        act, dall, tall, ig, *more = pl.pallas_call(
+            functools.partial(kernel, S, R, NH, Q),
+            out_shape=tuple(out_shape),
             in_specs=[anywhere] * 3,
-            out_specs=(anywhere, anywhere, anywhere, pl.BlockSpec(memory_space=pltpu.VMEM)),
-            scratch_shapes=[
-                pltpu.VMEM((F, H), BF),
-                pltpu.VMEM((S, T, F), BF),
-                pltpu.VMEM((S, m, H), BF),
-                pltpu.VMEM((J, R, m, ck), BF),
-                pltpu.VMEM((J, R + 1, m, ck), BF),
-                pltpu.VMEM((J, R, m, ck), BF),
-                pltpu.VMEM((J, m, ck), BF),
-                pltpu.VMEM((m, ck), F32),
-                pltpu.VMEM((T, F), F32),
-                pltpu.VMEM((T, F), F32),
-                pltpu.VMEM((S, T, F), BF),
-                pltpu.VMEM((S, T, F), BF),
-                dma((NH,)),
-                dma((2,)),
-                dma((S,)), dma((S,)), dma((S,)), dma((S,)),
-                dma((J, R)), dma((J, R + 1)), dma((J, R + 1)), dma((J, R)),
-                dma((J,)), dma((J,)), dma((J,)), dma((S,)),
-                dma((S,)), dma((S,)),
-            ],
+            out_specs=tuple(out_specs),
+            scratch_shapes=scratch,
             compiler_params=pltpu.CompilerParams(
                 collective_id=0, has_side_effects=True, vmem_limit_bytes=60 * 1024 * 1024
             ),
@@ -407,9 +500,12 @@
         else:
             total = lax.psum(ig, "col")
         grad = lax.dot_general(
-            dall.reshape(S * T, H), tall.reshape(S * T, F), (((0,), (0,)), ((), ())), preferred_element_type=F32
-        ).astype(BF)
-        return act, total, grad
+            dall.reshape(S * U, H), tall.reshape(S * U, F), (((0,), (0,)), ((), ())), preferred_element_type=F32
+        )
+        if Q > 1:
+            total = jnp.stack([more[0].reshape(R, m, F), total.reshape(R, m, F)], axis=1).reshape(T, F)
+            grad = grad + more[1].astype(F32)
+        return act, total, grad.astype(BF)
 
     in_specs = (P("seq", "row"), P("row", "col"), P(("seq", "row"), "col"))
     out_specs = (P(("seq", "row"), "col"), P("seq", "row"), P(("col", "seq"), "row"))

time: 110 us -> 127 us (1.15)
  Pallas kernels: 95.2 us -> 109 us
  starting transfers between devices: 1.55 us -> 4.28 us
  matrix products: 9.47 us -> 10.9 us
    pallas_call x1, Pallas kernels: 95.2 us -> 109 us  [shards(): pl.pallas_call(functools.partial(kernel, S, R, NH, Q), out_shape=tuple(ou...]
    ppermute x1, starting transfers between devices: 1.55 us -> 4.28 us  [shards(): other = lax.ppermute(ig, 'col', [(0, 1), (1, 0)])]
    dot_general x1, matrix products: 9.47 us -> 10.9 us  [shards(): lax.dot_general(dall.reshape(S * U, H), tall.reshape(S * U, F), (((0,), (...]
  transfers between devices with their start and end apart: 1 -> 1, of which waited for: 1 -> 0; matrix products, arithmetic and copies ran while one was open for 9% -> 9% of each run, Pallas kernels for 0% -> 0%
where the time goes in v1:
time: 127 us
  Pallas kernels  109 us (86%)
  matrix products  10.9 us (9%)
  starting transfers between devices  4.28 us (3%)
  local copies, waits for them, and re-layouts  1.66 us (1%)
    pallas_call x1, Pallas kernels, shards(): pl.pallas_call(functools.partial(kernel, S, R, NH, Q), out_shape=tuple(ou...  109 us
    dot_general x1, matrix products, shards(): lax.dot_general(dall.reshape(S * U, H), tall.reshape(S * U, F), (((0,), (...  10.9 us
    ppermute x1, starting transfers between devices, shards(): other = lax.ppermute(ig, 'col', [(0, 1), (1, 0)])  4.28 us
  transfers between devices with their start and end apart: 1, of which 0 were waited for; matrix products, arithmetic and copies ran while one was open for 9% of the time, Pallas kernels for 0%

profile of v1, /device:TPU:0, one launch (start us, length us, event | category | flops | bytes accessed | tf_op | source)
XLA Modules:
  0.0 127.0 jit_solution(10113997600237892864)
XLA Ops:
  0.6 109.4 %shard_map.58 = (bf16[32,12288]{1,0:T(8,128)(2,1)}, bf16[4,4,16,3072]{3,2,1,0:T(8,128)(2,1)}, bf16[4,64,1536]{2,1,0:T(8,128)(2,1)}, bf16[64,1536]{1,0:T(8,128)(2...) custom-call(bf16[128,1536]{1,0:T(8,128)(2,1)} %refs_0_.1, bf16[1536,12288]{1,0:T(8,128)(2,1)} %refs_1_.1, ...), custom_call_target="tpu_custom_call" | custom-call | tf_op jit(solution)/shard_map/pallas_call | solution.py:487
  110.1 4.3 %collective-permute-start = (bf16[64,1536]{1,0:T(8,128)(2,1)}, bf16[64,1536]{1,0:T(8,128)(2,1)S(1)}, u32[]{:S(2)}, u32[]{:S(2)}) collective-permute-start(bf16[64,1536]{1,0:T(8,128)(2,1)} %get-tuple-element.11), channel_id=1, source_target_pairs={{0,1},{1,0},{2,3},{3,2},{4,5},{5,4},{6,7},{7,6},{8,9},{9,8},{10,11... | collective-permute-start | bytes 589832 | tf_op jit(solution)/shard_map/ppermute | solution.py:498
  114.4 0.0 copy-start.2
  114.4 0.0 copy-start.1
  114.4 0.0 copy-start
  114.4 10.9 %add_convert_fusion = bf16[3072,1536]{1,0:T(8,128)(2,1)} fusion(bf16[3072,1536]{1,0:T(8,128)(2,1)} %get-tuple-element.14, bf16[256,3072]{1,0:T(8,128)(2,1)} %bitcast.7, bf16[256,1536]{1,0:T(8,128)(2,1)} %bitcast.9), kind=kOutput, calls=%fused_computation | convolution fusion | flops 2430074880 | bytes 21233664 | tf_op jit(solution)/shard_map/dot_general | solution.py:502
  125.2 0.0 collective-permute-done
  125.2 0.0 copy-done.2
  125.3 0.0 copy-done.1
  125.4 0.8 copy.6
  126.1 0.0 copy-done
  126.1 0.9 copy.8
  (2 shorter events, 0.1 us)
Async XLA Ops:
  110.1 15.2 %collective-permute-start = (bf16[64,1536]{1,0:T(8,128)(2,1)}, bf16[64,1536]{1,0:T(8,128)(2,1)S(1)}, u32[]{:S(2)}, u32[]{:S(2)}) collective-permute-start(bf16[64,1536]{1,0:T(8,128)(2,1)} %get-tuple-element.11), channel_id=1, source_target_pairs={{0,1},{1,0},{2,3},{3,2},{4,5},{5,4},{6,7},{7,6},{8,9},{9,8},{10,11... | collective-permute-start | bytes 589832 | tf_op jit(solution)/shard_map/ppermute | solution.py:498
  114.4 10.9 %copy-start.2 = (bf16[64,1536]{1,0:T(8,128)(2,1)S(1)}, bf16[64,1536]{1,0:T(8,128)(2,1)}, u32[]{:S(2)}) copy-start(bf16[64,1536]{1,0:T(8,128)(2,1)} %get-tuple-element.11) | copy-start | bytes 589828
  114.4 11.0 %copy-start.1 = (bf16[64,1536]{1,0:T(8,128)(2,1)S(1)}, bf16[64,1536]{1,0:T(8,128)(2,1)}, u32[]{:S(2)}) copy-start(bf16[64,1536]{1,0:T(8,128)(2,1)} %get-tuple-element.10) | copy-start | bytes 589828
  114.4 11.8 %copy-start = (bf16[32,12288]{1,0:T(8,128)(2,1)S(1)}, bf16[32,12288]{1,0:T(8,128)(2,1)}, u32[]{:S(2)}) copy-start(bf16[32,12288]{1,0:T(8,128)(2,1)} %get-tuple-element.18) | copy-start | bytes 2359300

commit v2 on v0

--- a/solution.py
+++ b/solution.py
@@ -46,6 +46,14 @@
     def cols(group, h=0, size=H):
         return pl.ds(pl.multiple_of(group * H + h * ck, 128), size)
 
+    def unit(j):
+        if NH == 1:
+            return j, 0
+        e = j - (NH - 1)
+        mine = (e < 0) | (e >= (S - 1) * NH)
+        k = jnp.where(mine, 0, 1 + jnp.maximum(e, 0) // NH)
+        return k, jnp.where(mine, jnp.where(e < 0, j, NH - 1), jnp.maximum(e, 0) % NH)
+
     right, left = lax.rem(r + 1, R), lax.rem(r + R - 1, R)
 
     wcopy = [pltpu.make_async_copy(w.at[:, cols(s, h, ck)], wv.at[:, pl.ds(h * ck, ck)], wsem.at[h]) for h in range(NH)]
@@ -125,17 +133,16 @@
     ftile = 512 if F % 512 == 0 else 128
 
     def project(j):
-        k, h = j // NH, j % NH
-
-        @pl.when(k == 0)
-        def _():
-            @pl.when(h == 0)
-            def _():
-                own_tok.wait()
-            for i in range(NH):
-                @pl.when(h == i)
-                def _():
-                    wcopy[i].wait()
+        k, h = unit(j)
+
+        @pl.when((k == 0) & (h == 0))
+        def _():
+            own_tok.wait()
+
+        for i in range(NH):
+            @pl.when((k == (1 if i and i == NH - 1 else 0)) & (h == i))
+            def _():
+                wcopy[i].wait()
 
         @pl.when((k > 0) & (h == 0))
         def _():
@@ -185,7 +192,7 @@
         each(R - 1, go)
 
     def finish(j):
-        k, h = j // NH, j % NH
+        k, h = unit(j)
         pre[...] = part[j, r].astype(F32)
 
         @pl.when(r > 0)
@@ -254,7 +261,7 @@
         each(R, go)
 
     def pull(j):
-        k, h = j // NH, j % NH
+        k, h = unit(j)
         dall_copy(j, k, h).start()
 
         def features(i):
@@ -268,24 +275,34 @@
                 preferred_element_type=F32,
             )
 
-            @pl.when(h == 0)
+            @pl.when((k == 0) & (h == 0))
+            def _():
+                igown[:, here] = value
+
+            @pl.when((k == 0) & (h > 0))
+            def _():
+                igown[:, here] += value
+
+            @pl.when((k > 0) & (h == 0))
             def _():
                 igacc[:, here] = value
 
-            @pl.when(h > 0)
+            @pl.when((k > 0) & (h > 0))
             def _():
                 igacc[:, here] += value
 
         each(F // ftile, features)
-
-        @pl.when((h == NH - 1) & (k == 0))
-        def _():
-            igown[...] = igacc[...]
 
         @pl.when((h == NH - 1) & (k > 0))
         def _():
             igs[k] = igacc[...].astype(BF)
             ig_copy(k).start()
+
+        @pl.when((h == NH - 1) & (k == S - 1))
+        def _():
+            for i in range(1, S - 1):
+                ig_copy(i).wait_recv()
+                igown[...] += igr[i].astype(F32)
 
     def at_step(j, ok, fn):
         @pl.when(ok & (j >= 0) & (j < J))
@@ -302,10 +319,8 @@
 
     each(J + LAG * 2 * (R - 1) + 1, step)
 
-    for k in range(1, S):
-        ig_copy(k).wait_recv()
-        igown[...] += igr[k].astype(F32)
-    ig[...] = igown[...].astype(BF)
+    ig_copy(S - 1).wait_recv()
+    ig[...] = (igown[...] + igr[S - 1].astype(F32)).astype(BF)
 
     for k in range(1, S):
         tok_copy(k).wait_send()
@@ -315,7 +330,7 @@
         tall_copy(k).wait()
 
     def drain(j):
-        k, h = j // NH, j % NH
+        k, h = unit(j)
         dall_copy(j, k, h).wait()
 
         @pl.when(k == 0)
@@ -354,6 +369,42 @@
             d_left(j, r).wait_send()
 
     each(J, drain)
+
+
+def weight_kernel(sub, grads, toks, act, grad, act_out):
+    act_out[...] = act[...]
+
+    def go(i, carry):
+        here = pl.ds(pl.multiple_of(i * sub, 128), sub)
+        grad[:, here] = lax.dot_general(
+            grads[...], toks[:, here], (((0,), (0,)), ((), ())), preferred_element_type=F32
+        ).astype(BF)
+        return carry
+
+    lax.fori_loop(0, grad.shape[1] // sub, go, 0)
+
+
+def weight_grad(grads, toks, act):
+    K, H = grads.shape
+    F = toks.shape[1]
+    m, width = act.shape
+    tm = next(n for n in (512, 384, 128) if H % n == 0)
+    n = H // tm
+    return pl.pallas_call(
+        functools.partial(weight_kernel, F),
+        out_shape=(jax.ShapeDtypeStruct((H, F), BF), jax.ShapeDtypeStruct((m, width), BF)),
+        grid=(n,),
+        in_specs=[
+            pl.BlockSpec((K, tm), lambda i: (0, i)),
+            pl.BlockSpec((K, F), lambda i: (0, 0), pipeline_mode=pl.Buffered(1)),
+            pl.BlockSpec((m, width // n), lambda i: (0, i)),
+        ],
+        out_specs=(pl.BlockSpec((tm, F), lambda i: (i, 0)), pl.BlockSpec((m, width // n), lambda i: (0, i))),
+        compiler_params=pltpu.CompilerParams(vmem_limit_bytes=24 * 1024 * 1024),
+        cost_estimate=pl.CostEstimate(
+            flops=2 * K * H * F, bytes_accessed=2 * (K * H + K * F + H * F + 2 * m * width), transcendentals=0
+        ),
+    )(grads, toks, act)
 
 
 def solution(mesh):
@@ -363,7 +414,7 @@
         T, F = tokens.shape
         H = weight.shape[1] // S
         m = cotangent.shape[0]
-        NH = next(n for n in (3, 1) if n == 1 or (H % (n * 128) == 0 and H >= 512 * n))
+        NH = next(n for n in (4, 1) if n == 1 or (H % (n * 128) == 0 and H >= 512 * n))
         J, ck = S * NH, H // NH
         dma = pltpu.SemaphoreType.DMA
         anywhere = pl.BlockSpec(memory_space=pl.ANY)
@@ -398,17 +449,15 @@
                 dma((S,)), dma((S,)),
             ],
             compiler_params=pltpu.CompilerParams(
-                collective_id=0, has_side_effects=True, vmem_limit_bytes=60 * 1024 * 1024
+                collective_id=0, has_side_effects=True, vmem_limit_bytes=40 * 1024 * 1024
             ),
-        )(tokens, weight, cotangent)
+        )(*[pltpu.with_memory_space_constraint(x, pltpu.HBM) for x in (tokens, weight, cotangent)])
         if C == 2:
             other = lax.ppermute(ig, "col", [(0, 1), (1, 0)])
             total = (ig.astype(F32) + other.astype(F32)).astype(BF)
         else:
             total = lax.psum(ig, "col")
-        grad = lax.dot_general(
-            dall.reshape(S * T, H), tall.reshape(S * T, F), (((0,), (0,)), ((), ())), preferred_element_type=F32
-        ).astype(BF)
+        grad, act = weight_grad(dall.reshape(S * T, H), tall.reshape(S * T, F), act)
         return act, total, grad
 
     in_specs = (P("seq", "row"), P("row", "col"), P(("seq", "row"), "col"))

time: 110 us -> 106 us (0.964)
  matrix products: 9.47 us -> 0 us
  Pallas kernels: 95.2 us -> 103 us
    dot_general x1 -> x0, matrix products: 9.47 us -> none  [shards(): lax.dot_general(dall.reshape(S * T, H), tall.reshape(S * T, F), (((0,), (...]
    pallas_call x0 -> x1, Pallas kernels: none -> 7.71 us  [weight_grad(): pl.pallas_call(functools.partial(weight_kernel, F), out_shape=(jax.ShapeD...]
  transfers between devices with their start and end apart: 1 -> 1, of which waited for: 1 -> 1; matrix products, arithmetic and copies ran while one was open for 9% -> 0% of each run, Pallas kernels for 0% -> 7%
where the time goes in v2:
time: 106 us
  Pallas kernels  103 us (97%)
  starting transfers between devices  1.55 us (1%)
    pallas_call x1, Pallas kernels, shards(): pl.pallas_call(functools.partial(kernel, S, R, NH), out_shape=(jax.ShapeD...  95.3 us
    pallas_call x1, Pallas kernels, weight_grad(): pl.pallas_call(functools.partial(weight_kernel, F), out_shape=(jax.ShapeD...  7.71 us
  transfers between devices with their start and end apart: 1, of which 1 were waited for; matrix products, arithmetic and copies ran while one was open for 0% of the time, Pallas kernels for 7%

profile of v2, /device:TPU:0, one launch (start us, length us, event | category | flops | bytes accessed | tf_op | source)
XLA Modules:
  0.0 106.2 jit_solution(15469031753530852978)
XLA Ops:
  0.6 95.3 %shard_map.58 = (bf16[32,12288]{1,0:T(8,128)(2,1)S(1)}, bf16[4,4,32,3072]{3,2,1,0:T(8,128)(2,1)S(1)}, bf16[4,128,1536]{2,1,0:T(8,128)(2,1)S(1)}, bf16[128,1536]{1,0:T(8,128)(2,1)S(1)}) custom-call(bf16[128,1536]{1,0:T(8,128)(2,1)} %tok.1, bf16[1536,12288]{1,0:T(8,128)(2,1)} %w.1, bf16[32,12288]{1,0:T(8,128)(2,1)} %cot.1), custom_call_target="tpu_custom_call" | custom-call | tf_op jit(solution)/shard_map/pallas_call | solution.py:421
  95.9 1.5 %collective-permute-start = (bf16[128,1536]{1,0:T(8,128)(2,1)S(1)}, bf16[128,1536]{1,0:T(8,128)(2,1)S(1)}, u32[]{:S(2)}, u32[]{:S(2)}) collective-permute-start(bf16[128,1536]{1,0:T(8,128)(2,1)S(1)} %get-tuple-element.13), channel_id=1, source_target_pairs={{0,1},{1,0},{2,3},{3,2},{4,5},{5,4},{6,7},{7,6},{8,9},{9,8},{10,11... | collective-permute-start | bytes 1179656 | tf_op jit(solution)/shard_map/ppermute | solution.py:456
  97.5 7.7 %shard_map.59 = (bf16[3072,1536]{1,0:T(8,128)(2,1)}, bf16[32,12288]{1,0:T(8,128)(2,1)}) custom-call(bf16[512,3072]{1,0:T(8,128)(2,1)S(1)} %bitcast.2, bf16[512,1536]{1,0:T(8,128)(2,1)S(1)} %bitcast.3, bf16[32,12288]{1,0:T(8,128)(2,1)S(1)} %get-tuple-element.11.act), custom_call_target="tpu_custom_call" | custom-call | flops 4831838208 | bytes 15728640 | tf_op jit(solution)/shard_map/pallas_call | solution.py:393
  105.2 0.2 collective-permute-done
  105.4 0.8 add_convert_fusion
Async XLA Ops:
  95.9 9.5 %collective-permute-start = (bf16[128,1536]{1,0:T(8,128)(2,1)S(1)}, bf16[128,1536]{1,0:T(8,128)(2,1)S(1)}, u32[]{:S(2)}, u32[]{:S(2)}) collective-permute-start(bf16[128,1536]{1,0:T(8,128)(2,1)S(1)} %get-tuple-element.13), channel_id=1, source_target_pairs={{0,1},{1,0},{2,3},{3,2},{4,5},{5,4},{6,7},{7,6},{8,9},{9,8},{10,11... | collective-permute-start | bytes 1179656 | tf_op jit(solution)/shard_map/ppermute | solution.py:456

commit v3 on v2

--- a/solution.py
+++ b/solution.py
@@ -304,6 +304,45 @@
                 ig_copy(i).wait_recv()
                 igown[...] += igr[i].astype(F32)
 
+    def drain(j):
+        k, h = unit(j)
+        dall_copy(j, k, h).wait()
+
+        @pl.when(k == 0)
+        def _():
+            act_local(j, h).wait()
+
+        @pl.when(k > 0)
+        def _():
+            act_remote(j, k, h).wait()
+
+        def block(o):
+            @pl.when(o > r)
+            def _():
+                sum_right(j, o).wait_send()
+
+                @pl.when(r > 0)
+                def _():
+                    d_left(j, o).wait_send()
+
+            @pl.when(o < r)
+            def _():
+                sum_left(j, o).wait_send()
+
+                @pl.when(r < R - 1)
+                def _():
+                    d_right(j, o).wait_send()
+
+        each(R, block)
+
+        @pl.when(r < R - 1)
+        def _():
+            d_right(j, r).wait_send()
+
+        @pl.when(r > 0)
+        def _():
+            d_left(j, r).wait_send()
+
     def at_step(j, ok, fn):
         @pl.when(ok & (j >= 0) & (j < J))
         def _():
@@ -316,6 +355,7 @@
         at_step(t - LAG * (R - 1 - r), r < R - 1, add_left)
         at_step(t - LAG * far(r), True, finish)
         relay(t)
+        at_step(t - LAG * 2 * (R - 1) - 3, True, drain)
 
     each(J + LAG * 2 * (R - 1) + 1, step)
 
@@ -329,46 +369,8 @@
     for k in range(S):
         tall_copy(k).wait()
 
-    def drain(j):
-        k, h = unit(j)
-        dall_copy(j, k, h).wait()
-
-        @pl.when(k == 0)
-        def _():
-            act_local(j, h).wait()
-
-        @pl.when(k > 0)
-        def _():
-            act_remote(j, k, h).wait()
-
-        def block(o):
-            @pl.when(o > r)
-            def _():
-                sum_right(j, o).wait_send()
-
-                @pl.when(r > 0)
-                def _():
-                    d_left(j, o).wait_send()
-
-            @pl.when(o < r)
-            def _():
-                sum_left(j, o).wait_send()
-
-                @pl.when(r < R - 1)
-                def _():
-                    d_right(j, o).wait_send()
-
-        each(R, block)
-
-        @pl.when(r < R - 1)
-        def _():
-            d_right(j, r).wait_send()
-
-        @pl.when(r > 0)
-        def _():
-            d_left(j, r).wait_send()
-
-    each(J, drain)
+    done = max(J - 2, 0)
+    each(J - done, lambda i: drain(done + i))
 
 
 def weight_kernel(sub, grads, toks, act, grad, act_out):

time: 106 us -> 105 us (level)
  no operation moved by 1% of the time
where the time goes in v3:
time: 105 us
  Pallas kernels  102 us (97%)
  starting transfers between devices  1.59 us (2%)
    pallas_call x1, Pallas kernels, shards(): pl.pallas_call(functools.partial(kernel, S, R, NH), out_shape=(jax.ShapeD...  94.3 us
    pallas_call x1, Pallas kernels, weight_grad(): pl.pallas_call(functools.partial(weight_kernel, F), out_shape=(jax.ShapeD...  7.71 us
  transfers between devices with their start and end apart: 1, of which 1 were waited for; matrix products, arithmetic and copies ran while one was open for 0% of the time, Pallas kernels for 7%

profile of v3, /device:TPU:0, one launch (start us, length us, event | category | flops | bytes accessed | tf_op | source)
XLA Modules:
  0.0 105.2 jit_solution(16748924446625182507)
XLA Ops:
  0.6 94.3 %shard_map.58 = (bf16[32,12288]{1,0:T(8,128)(2,1)S(1)}, bf16[4,4,32,3072]{3,2,1,0:T(8,128)(2,1)S(1)}, bf16[4,128,1536]{2,1,0:T(8,128)(2,1)S(1)}, bf16[128,1536]{1,0:T(8,128)(2,1)S(1)}) custom-call(bf16[128,1536]{1,0:T(8,128)(2,1)} %tok.1, bf16[1536,12288]{1,0:T(8,128)(2,1)} %w.1, bf16[32,12288]{1,0:T(8,128)(2,1)} %cot.1), custom_call_target="tpu_custom_call" | custom-call | tf_op jit(solution)/shard_map/pallas_call | solution.py:423
  95.0 1.6 %collective-permute-start = (bf16[128,1536]{1,0:T(8,128)(2,1)S(1)}, bf16[128,1536]{1,0:T(8,128)(2,1)S(1)}, u32[]{:S(2)}, u32[]{:S(2)}) collective-permute-start(bf16[128,1536]{1,0:T(8,128)(2,1)S(1)} %get-tuple-element.13), channel_id=1, source_target_pairs={{0,1},{1,0},{2,3},{3,2},{4,5},{5,4},{6,7},{7,6},{8,9},{9,8},{10,11... | collective-permute-start | bytes 1179656 | tf_op jit(solution)/shard_map/ppermute | solution.py:458
  96.6 7.7 %shard_map.59 = (bf16[3072,1536]{1,0:T(8,128)(2,1)}, bf16[32,12288]{1,0:T(8,128)(2,1)}) custom-call(bf16[512,3072]{1,0:T(8,128)(2,1)S(1)} %bitcast.2, bf16[512,1536]{1,0:T(8,128)(2,1)S(1)} %bitcast.3, bf16[32,12288]{1,0:T(8,128)(2,1)S(1)} %get-tuple-element.11.act), custom_call_target="tpu_custom_call" | custom-call | flops 4831838208 | bytes 15728640 | tf_op jit(solution)/shard_map/pallas_call | solution.py:395
  104.3 0.1 collective-permute-done
  104.4 0.8 add_convert_fusion
Async XLA Ops:
  95.0 9.4 %collective-permute-start = (bf16[128,1536]{1,0:T(8,128)(2,1)S(1)}, bf16[128,1536]{1,0:T(8,128)(2,1)S(1)}, u32[]{:S(2)}, u32[]{:S(2)}) collective-permute-start(bf16[128,1536]{1,0:T(8,128)(2,1)S(1)} %get-tuple-element.13), channel_id=1, source_target_pairs={{0,1},{1,0},{2,3},{3,2},{4,5},{5,4},{6,7},{7,6},{8,9},{9,8},{10,11... | collective-permute-start | bytes 1179656 | tf_op jit(solution)/shard_map/ppermute | solution.py:458
